TPU v7x, 512 devices: a whole 4x8x8 slice. The times are simulated.
512 devices in a mesh: samp: 64 (over z, y_hi, core), var: 8 (over x, y_lo).
Axes of the slice: x: 4, y: 8 (y_hi: 4, y_lo: 2; y = y_hi * 2 + y_lo), z: 8, core: 2. Of those that a mesh axis runs over, the one named last changes fastest.
Arguments:
- dosages: bfloat16 [32768, 14336], P('samp', 'var'), may hold values from 0 to 2
- weights: bfloat16 [14336, 512], P('var'), may hold values from -0.046875 to 0.046875
- prior: float32 [32768, 512], P('samp', 'var'), may hold values from -16 to 16
- cohort: int32 [32768, 1], P('samp'), may hold values from 0 to 15
- expression: bfloat16 [32768, 10240], P('samp', 'var'), may hold values from -6 to 6
Outputs:
- correlation: float32 [512, 10240], P('samp', 'var')
Inputs may be any that keep to these rules, and one draw needn't show every extreme that they name: Every cohort has at least one sample.
All inputs are finite; a program needn't handle non-finite values.
Results may differ from a plain program's by a relative error of at most 0.0042.
Values may be sent and summed in bfloat16 or wider, within the bound.
A program may use at most 64 MiB of HBM per device.

v0:
```python
import jax
import jax.numpy as jnp
from jax import lax
from jax.sharding import PartitionSpec as P

COHORTS = 16


def filled_up(lines, peers):
    spare = -lines.shape[0] % peers
    if not spare:
        return lines
    return jnp.concatenate([lines, jnp.zeros((spare, *lines.shape[1:]), lines.dtype)])


def sent_to_all(x, axis):
    peers = lax.axis_size(axis)
    return lax.all_to_all(jnp.broadcast_to(x[None], (peers, *x.shape)), axis, 0, 0, tiled=True)


def laid_out(parts, dim):
    parts = jnp.moveaxis(parts, 0, dim)
    lengths = parts.shape
    return parts.reshape(*lengths[:dim], lengths[dim] * lengths[dim + 1], *lengths[dim + 2 :])


def gathered_copies(x, axis, dim):
    parts = sent_to_all(x, axis)
    return laid_out(parts, dim)


def split_up(x, dim, peers):
    lengths = x.shape
    parts = x.reshape(*lengths[:dim], peers, lengths[dim] // peers, *lengths[dim + 1 :])
    return jnp.moveaxis(parts, dim, 0)


def summed_on_arrival(x, axis, dim):
    parts = split_up(x, dim, lax.axis_size(axis))
    arrived = lax.all_to_all(parts, axis, split_axis=0, concat_axis=0, tiled=True)
    return arrived.sum(axis=0)


def total_of(x, axes):
    padded = filled_up(x, lax.axis_size(axes))
    whole = gathered_copies(summed_on_arrival(padded, axes, 0), axes, 0)
    return lax.slice_in_dim(whole, 0, len(x)).reshape(x.shape)


def together(arrays, axis):
    ravelled, at, gathered = (jnp.concatenate([a.reshape(-1) for a in arrays]), 0, [])
    so_far = total_of(ravelled, axis)
    for a in arrays:
        gathered.append(so_far[at : at + a.size].reshape(a.shape))
        at += a.size
    return tuple(gathered)


def summed_on_arrival_2(x, axis, dim):
    parts = split_up(x, dim, lax.axis_size(axis))
    arrived = lax.all_to_all(parts, axis, split_axis=0, concat_axis=0, tiled=True)
    return arrived.astype(jnp.float32).sum(axis=0)


def standardize(scores, onehot):
    sums = jnp.dot(onehot.T, scores, precision=lax.Precision.HIGHEST)
    counts = jnp.sum(onehot, axis=0)
    raw_squares = jnp.sum(scores * scores, axis=0)
    sums, counts, raw_squares = together((sums, counts, raw_squares), "samp")
    means = sums / counts[:, None]
    centered = scores - jnp.dot(onehot, means, precision=lax.Precision.HIGHEST)
    squares = raw_squares - jnp.sum(sums * means, axis=0)
    total = jnp.sum(counts)
    spread = lax.rsqrt(squares / total + 1e-06)
    return ((centered * spread[None, :]).astype(jnp.bfloat16), total)


def shards(dosages, weights, prior, cohort, expression):
    width = prior.shape[1]
    offset = lax.axis_index("var") * width
    partial_value = jnp.dot(dosages, weights, preferred_element_type=jnp.float32)
    own_part = lax.dynamic_slice_in_dim(partial_value, offset, width, 1) + prior
    partial_value = lax.dynamic_update_slice_in_dim(partial_value, own_part, offset, 1)
    onehot = (cohort == jnp.arange(COHORTS, dtype=jnp.int32)[None, :]).astype(jnp.float32)
    shares = summed_on_arrival(partial_value, "var", 1)
    standard_share, total = standardize(shares, onehot)
    standard = gathered_copies(standard_share, "var", 1)
    cross = summed_on_arrival_2(
        lax.dot_general(
            standard, expression, (((0,), (0,)), ((), ())), preferred_element_type=jnp.float32
        ).astype(jnp.bfloat16),
        "samp",
        0,
    )
    return cross / total


def solution(mesh):
    placed = (P("samp", "var"), P("var", None), P("samp", "var"), P("samp", None), P("samp", "var"))
    return jax.shard_map(
        shards, mesh=mesh, in_specs=placed, out_specs=P("samp", "var"), check_vma=False
    )
```

profile of v0, /device:TPU:1, one launch (start us, length us, event | category | flops | bytes accessed | tf_op | source)
XLA Modules:
  0.0 132.7 jit_solution(2377452254443003842)
XLA Ops:
  0.0 0.0 copy-start
  0.0 1.5 %copy-done = bf16[512,1792]{1,0:T(8,128)(2,1)S(1)} copy-done((bf16[512,1792]{1,0:T(8,128)(2,1)S(1)}, bf16[512,1792]{1,0:T(8,128)(2,1)}, u32[]{:S(2)}) %copy-start) | copy-done | bytes 1835032
  1.5 0.0 copy-start.2
  1.5 2.7 %fusion.7 = f32[512,512]{0,1:T(8,128)S(1)} fusion(bf16[512,1792]{1,0:T(8,128)(2,1)S(1)} %copy-done, bf16[1792,512]{1,0:T(8,128)(2,1)} %param.6), kind=kOutput, calls=%fused_computation.20 | convolution fusion | flops 939524096 | bytes 4718592 | tf_op jit(solution)/shard_map/dot_general | solution.py:81
  4.2 0.0 copy-done.2
  4.2 0.0 copy-start.3
  4.3 0.0 copy-start.1
  4.3 1.0 copy-done.1
  5.3 5.8 %all-to-all-start = ((f32[8,512,64]{1,2,0:T(8,128)}), f32[8,512,64]{1,2,0:T(8,128)S(1)}, u32[]{:S(2)}, u32[]{:S(2)}) async-start(f32[8,512,64]{1,2,0:T(8,128)} %bitcast.16), calls=%async_computation | async-start | bytes 2097152 | tf_op jit(solution)/shard_map/all_to_all | solution.py:40
  11.1 0.0 copy-done.3
  11.1 0.1 convert_reduce_fusion.1
  11.2 11.0 %all-to-all-done = f32[8,512,64]{1,2,0:T(8,128)S(1)} async-done(((f32[8,512,64]{1,2,0:T(8,128)}), f32[8,512,64]{1,2,0:T(8,128)S(1)}, u32[]{:S(2)}, u32[]{:S(2)}) %all-to-all-start) | async-done | bytes 1048608 | tf_op jit(solution)/shard_map/all_to_all | solution.py:40
  22.2 0.1 reduce_sum.63
  22.3 0.0 copy-start.4
  22.3 0.1 multiply_reduce_fusion
  22.4 0.1 fusion.3
  22.6 0.1 reshape.33
  22.6 0.1 concatenate.3
  22.7 0.2 all_to_all.20
  22.9 32.4 %all_to_all.30 = f32[64,1,18]{2,1,0:T(1,128)S(1)} all-to-all(f32[64,1,18]{2,1,0:T(1,128)S(1)} %bitcast.19), channel_id=1, replica_groups=mesh['samp'=64,'var'=8] {'samp'}, dimensions={0} | all-to-all | bytes 9216 | tf_op jit(solution)/shard_map/all_to_all | solution.py:40
  55.3 0.1 reduce_sum.66
  55.4 15.8 %all_to_all.31 = f32[64,1,18]{2,1,0:T(1,128)S(1)} all-to-all(f32[64,1,18]{2,1,0:T(1,128)S(1)} %broadcast_in_dim.7), channel_id=1, replica_groups=mesh['samp'=64,'var'=8] {'samp'}, dimensions={0} | all-to-all | bytes 9216 | tf_op jit(solution)/shard_map/all_to_all | solution.py:18
  71.2 0.1 reshape.34
  71.3 0.7 slice_reduce_fusion
  72.0 0.5 broadcast.11
  72.5 0.7 reduce.6
  73.3 0.1 slice.16
  73.4 0.1 multiply_reduce_fusion.1
  73.5 0.8 add_rsqrt_fusion
  74.2 0.3 fusion.2
  74.6 11.6 %all_to_all.32 = bf16[8,512,64]{1,2,0:T(8,128)(2,1)S(1)} all-to-all(bf16[8,512,64]{1,2,0:T(8,128)(2,1)S(1)} %broadcast_in_dim.8), channel_id=1, replica_groups=mesh['samp'=64,'var'=8] {'var'}, dimensions={0} | all-to-all | bytes 1048576 | tf_op jit(solution)/shard_map/all_to_all | solution.py:18
  86.2 0.0 copy-done.4
  86.2 0.8 fusion
  87.1 44.1 %all_to_all.33 = bf16[64,8,1280]{2,1,0:T(8,128)(2,1)S(1)} all-to-all(bf16[64,8,1280]{2,1,0:T(8,128)(2,1)S(1)} %fusion), channel_id=1, replica_groups=mesh['samp'=64,'var'=8] {'samp'}, dimensions={0} | all-to-all | bytes 2621440 | tf_op jit(solution)/shard_map/all_to_all | solution.py:61
  131.1 0.2 convert_reduce_fusion
  131.4 1.3 broadcast_divide_fusion
  (4 shorter events, 0.1 us)
Async XLA Ops:
  0.0 1.5 %copy-start = (bf16[512,1792]{1,0:T(8,128)(2,1)S(1)}, bf16[512,1792]{1,0:T(8,128)(2,1)}, u32[]{:S(2)}) copy-start(bf16[512,1792]{1,0:T(8,128)(2,1)} %param.5) | copy-start | bytes 5505028
  1.5 2.7 %copy-start.2 = (f32[512,64]{0,1:T(8,128)S(1)}, f32[512,64]{0,1:T(8,128)}, u32[]{:S(2)}) copy-start(f32[512,64]{0,1:T(8,128)} %param.7) | copy-start | bytes 393220
  4.2 6.9 %copy-start.3 = (s32[512,1]{0,1:T(1,128)S(1)}, s32[512,1]{0,1:T(1,128)}, u32[]{:S(2)}) copy-start(s32[512,1]{0,1:T(1,128)} %param.8) | copy-start | bytes 6148
  4.3 1.0 copy-start.1
  5.3 16.9 %all-to-all-start = ((f32[8,512,64]{1,2,0:T(8,128)}), f32[8,512,64]{1,2,0:T(8,128)S(1)}, u32[]{:S(2)}, u32[]{:S(2)}) async-start(f32[8,512,64]{1,2,0:T(8,128)} %bitcast.16), calls=%async_computation | async-start | bytes 2097152 | tf_op jit(solution)/shard_map/all_to_all | solution.py:40
  22.3 63.9 %copy-start.4 = (bf16[512,1280]{1,0:T(8,128)(2,1)S(1)}, bf16[512,1280]{1,0:T(8,128)(2,1)}, u32[]{:S(2)}) copy-start(bf16[512,1280]{1,0:T(8,128)(2,1)} %param.9) | copy-start | bytes 3932164
where the time goes:
time: 133 us
  blocking collectives  104 us (78%)
  waiting for transfers between devices  11 us (8%)
  starting transfers between devices  5.85 us (4%)
  other arithmetic  4.21 us (3%)
  matrix products  4.01 us (3%)
  local copies, waits for them, and re-layouts  3.64 us (3%)
    all_to_all x1, blocking collectives, summed_on_arrival_2(): lax.all_to_all(parts, axis, split_axis=0, concat_axis=0, tiled=True)  44.1 us
    all_to_all x1, blocking collectives, summed_on_arrival(): lax.all_to_all(parts, axis, split_axis=0, concat_axis=0, tiled=True)  32.4 us
    all_to_all x2, blocking collectives, sent_to_all(): lax.all_to_all(jnp.broadcast_to(x[None], (peers, *x.shape)), axis, 0, 0,...  27.4 us
    all_to_all x1, waiting for transfers between devices, summed_on_arrival(): lax.all_to_all(parts, axis, split_axis=0, concat_axis=0, tiled=True)  11 us
    all_to_all x1, starting transfers between devices, summed_on_arrival(): lax.all_to_all(parts, axis, split_axis=0, concat_axis=0, tiled=True)  5.85 us
    dot_general x1, matrix products, shards(): jnp.dot(dosages, weights, preferred_element_type=jnp.float32)  2.69 us
  transfers between devices with their start and end apart: 1, of which 1 were waited for; matrix products, arithmetic and copies ran while one was open for 0% of the time, Pallas kernels for 0%

commit v1 on v0

v1 whole, which is shorter than its diff:
```python
import functools

import jax
import jax.numpy as jnp
from jax import lax
from jax.experimental import pallas as pl
from jax.experimental.pallas import tpu as pltpu
from jax.sharding import PartitionSpec as P

COHORTS = 16
MESH = pl.DeviceIdType.MESH
F32 = jnp.float32
BF16 = jnp.bfloat16
NX, NL, NZ, NY, NC = 4, 2, 8, 4, 2
VAR = [(dx, dl) for dx in (2, 1, 3, 0) for dl in (1, 0) if dx or dl]
YC = [(dy, dc) for dy in (2, 1, 3, 0) for dc in (1, 0) if dy or dc]
ZD = [4, 3, 5, 2, 6, 1, 7]


def split2(a):
    hi = a.astype(BF16)
    return hi, (a - hi.astype(F32)).astype(BF16)


def split3(a):
    hi = a.astype(BF16)
    rest = a - hi.astype(F32)
    mid = rest.astype(BF16)
    return hi, mid, (rest - mid.astype(F32)).astype(BF16)


def dot(a, b):
    return jnp.dot(a, b, preferred_element_type=F32)


def dot_t(a, b):
    return lax.dot_general(a, b, (((0,), (0,)), ((), ())), preferred_element_type=F32)


def dot_nt(a, b):
    return lax.dot_general(a, b, (((1,), (1,)), ((), ())), preferred_element_type=F32)


def kernel(
    total, d_hbm, w_hbm, p_hbm, co_hbm, e_hbm, o_ref,
    d, w, p, co, e_all, lt, rt, snd, own, rs_buf, x_all, st_src, st_buf, t_src, yc_buf, t2_src, z_buf,
    d_src, dm, cross, cb, zx_buf, ysrc, yx_buf, q_src, q_yc, q2_src, q_z,
    ld, e_sem, st_s, st_r, yc_s, yc_r, z_s, z_r, dm_s, dm_r, rs_s, rs_r, ag_s, ag_r, sb_s, sb_r,
    zx_s, zx_r, yx_s, yx_r, qy_s, qy_r, qz_s, qz_r,
):
    samp, var = lax.axis_index("samp"), lax.axis_index("var")
    z, y, c = samp // 8, (samp // 2) % 4, samp % 2
    x, l = var // 2, var % 2
    nv = NX * NL
    rows = d.shape[0]
    blk = rows // nv
    k = w.shape[1]
    half = e_all.shape[1]
    zrows = k // NZ

    def var_of(dx, dl):
        return ((x + dx) % NX) * NL + (l + dl) % NL

    def samp_of(dz, dy, dc):
        return ((z + dz) % NZ) * 8 + ((y + dy) % NY) * 2 + (c + dc) % NC

    sib = (samp_of(0, 0, 1), var)

    def remote(src, dst, ss, rs, dev):
        cp = pltpu.make_async_remote_copy(
            src_ref=src, dst_ref=dst, send_sem=ss, recv_sem=rs, device_id=dev, device_id_type=MESH
        )
        cp.start()
        return cp

    def local(src, dst, sem):
        cp = pltpu.make_async_copy(src, dst, sem)
        cp.start()
        return cp

    barrier = pltpu.get_barrier_semaphore()
    peers = (
        [(samp, var_of(*q)) for q in VAR]
        + [(samp_of(0, 0, 1), var_of(*q)) for q in VAR]
        + [(samp_of(0, *q), var) for q in YC]
        + [(samp_of(q, 0, 0), var) for q in ZD]
    )
    for dev in peers:
        pl.semaphore_signal(barrier, inc=1, device_id=dev, device_id_type=MESH)

    cp_co = local(co_hbm, co.at[0], ld.at[0])
    cp_d = local(d_hbm, d, ld.at[1])
    cp_w = local(w_hbm, w, ld.at[2])
    cp_p = local(p_hbm, p, ld.at[3])
    mine = pl.multiple_of(c * half, 128)
    other = pl.multiple_of((1 - c) * half, 128)
    cp_e = local(e_hbm.at[:, pl.ds(mine, half)], e_all.at[pl.ds(0, rows)], ld.at[4])

    cp_co.wait()
    cohorts = lax.broadcasted_iota(jnp.int32, (COHORTS, rows), 0)
    hot = (co[0] == cohorts).astype(F32)
    oh = hot.astype(BF16)
    count = jnp.sum(hot, axis=1, keepdims=True)
    cp_p.wait()
    p3 = split3(p[...])
    width = p.shape[0]
    for i in range(3):
        lt[i * width : (i + 1) * width] = p3[i]
        lt[3 * width + i * COHORTS : 3 * width + (i + 1) * COHORTS] = oh
    lt[3 * width + 3 * COHORTS :] = jnp.zeros((COHORTS, rows), BF16)
    sel = lax.broadcasted_iota(jnp.int32, (width, k), 1) - var * width == lax.broadcasted_iota(jnp.int32, (width, k), 0)
    sel = sel.astype(F32).astype(BF16)
    ps = [dot_nt(oh, p3[i]) for i in range(3)]
    ps = ps[0] + ps[1] + ps[2]
    ps = sum(dot(part, sel) for part in split3(ps))
    cp_d.wait()
    a3 = split3(dot(oh, d[...]))
    cp_w.wait()
    sums = ps + sum(dot(part, w[...]) for part in a3)
    m3 = split3(-sums / jnp.maximum(count, 1.0))
    for i in range(3):
        rt[i * width : (i + 1) * width] = sel
        rt[3 * width + i * COHORTS : 3 * width + (i + 1) * COHORTS] = m3[i]
    rt[3 * width + 3 * COHORTS :] = jnp.zeros((COHORTS, k), BF16)
    lane = lax.broadcasted_iota(jnp.int32, (COHORTS, 128), 1)
    low = lane < width
    for j in range(k // 128):
        pair = sums[:, j * 128 : (j + 1) * 128]
        st_src[2 * j] = jnp.where(low, pair, count)
        st_src[2 * j + 1] = jnp.where(low, pltpu.roll(pair, 64, 1), count)

    pl.semaphore_wait(barrier, len(peers))
    cp_e2 = remote(e_hbm.at[:, pl.ds(other, half)], e_all.at[pl.ds(rows, rows)], e_sem.at[0], e_sem.at[1], sib)
    cp_co2 = remote(co_hbm, co.at[1], e_sem.at[2], e_sem.at[3], sib)
    st = [
        remote(st_src.at[var_of(*q)], st_buf.at[i], st_s.at[i], st_r.at[i], (samp, var_of(*q)))
        for i, q in enumerate(VAR)
    ]

    rs = []
    for step, dx in enumerate((2, 1, 3, 0)):
        xo = (x + dx) % NX
        r0 = pl.multiple_of(xo * (2 * blk), 2 * blk)
        f = dot(d[pl.ds(r0, 2 * blk)], w[...]) + dot_t(lt[:, pl.ds(r0, 2 * blk)], rt[...])
        snd[pl.ds(r0, 2 * blk)] = f.astype(BF16)
        if dx == 0:
            own[...] = f
        for dl in (1, 0):
            if dx or dl:
                i = VAR.index((dx, dl))
                to = var_of(dx, dl)
                rs.append(
                    remote(
                        snd.at[pl.ds(pl.multiple_of(to * blk, blk), blk)], rs_buf.at[i], rs_s.at[i], rs_r.at[i],
                        (samp, to),
                    )
                )

    for cp in st:
        cp.wait_recv()
    t = st_src[var]
    for i in range(len(VAR)):
        t = t + st_buf[i]
    t = jnp.where(low, t, count)
    t_src[...] = t
    ycs = [
        remote(t_src, yc_buf.at[i], yc_s.at[i], yc_r.at[i], (samp_of(0, *q), var)) for i, q in enumerate(YC)
    ]
    cp_e.wait()
    e_own = dot(oh, e_all[pl.ds(0, rows)])
    cp_e2.wait_recv()
    cp_co2.wait_recv()
    oh2 = (co[1] == cohorts).astype(F32).astype(BF16)
    e_sib = dot(oh2, e_all[pl.ds(rows, rows)])

    for cp in rs:
        cp.wait_recv()
    at = pl.multiple_of(l * blk, blk)
    s = own[pl.ds(at, blk)]
    for i in range(len(VAR)):
        s = s + rs_buf[i].astype(F32)
    row = pl.multiple_of(var * blk, blk)
    x_all[pl.ds(row, blk)] = s.astype(BF16)
    ag = [
        remote(x_all.at[pl.ds(row, blk)], x_all.at[pl.ds(row, blk)], ag_s.at[i], ag_r.at[i], (samp, var_of(*q)))
        for i, q in enumerate(VAR)
    ]
    sb = [
        remote(x_all.at[pl.ds(row, blk)], x_all.at[pl.ds(pl.multiple_of(rows + row, blk), blk)], sb_s.at[7], sb_r.at[7], sib)
    ]

    for cp in ycs:
        cp.wait_recv()
    t2 = t
    for i in range(len(YC)):
        t2 = t2 + yc_buf[i]
    t2_src[...] = t2
    zs = [
        remote(t2_src, z_buf.at[i], z_s.at[i], z_r.at[i], (samp_of(q, 0, 0), var)) for i, q in enumerate(ZD)
    ]
    for i in range(len(VAR) - 1, -1, -1):
        dx, dl = VAR[i]
        ag[i].wait_recv()
        got = pl.multiple_of(var_of(-dx, -dl) * blk, blk)
        sb.append(
            remote(
                x_all.at[pl.ds(got, blk)], x_all.at[pl.ds(pl.multiple_of(rows + got, blk), blk)], sb_s.at[i], sb_r.at[i], sib
            )
        )
    for cp in zs:
        cp.wait_recv()
    t3 = t2
    for i in range(len(ZD)):
        t3 = t3 + z_buf[i]
    mean = t3 / pltpu.roll(t3, 64, 1)
    d_src[...] = jnp.where(low, t / jnp.maximum(count, 1.0) - mean, 0.0)
    dm[0, var] = d_src[...]
    dms = []
    for i, q in enumerate(VAR):
        for dc in range(NC):
            n = 2 * i + dc
            dms.append(
                remote(d_src, dm.at[dc, var], dm_s.at[n], dm_r.at[n], (samp_of(0, 0, dc), var_of(*q)))
            )
    dms.append(remote(d_src, dm.at[1, var], dm_s.at[14], dm_r.at[14], sib))

    for cp in sb:
        cp.wait_recv()
    cross[...] = dot_t(x_all[...], e_all[...])
    for cp in dms:
        cp.wait_recv()

    def spread_out(i):
        return jnp.concatenate(
            [jnp.where(low, dm[i, 2 * j], pltpu.roll(dm[i, 2 * j + 1], 64, 1)) for j in range(nv // 2)], axis=1
        )

    d_own = spread_out(0)
    d2 = [split2(d_own), split2(spread_out(1))]
    e2 = [split2(e_own), split2(e_sib)]
    left = jnp.concatenate([d2[i][a] for i in range(2) for a in range(2) for b in range(2)], axis=0)
    right = jnp.concatenate([e2[i][b] for i in range(2) for a in range(2) for b in range(2)], axis=0)
    full = cross[...] + dot_t(left, right)
    cross[...] = full
    cb[...] = full.astype(BF16)
    zx = []
    for i, q in enumerate(ZD):
        to = pl.multiple_of(((z + q) % NZ) * zrows, zrows)
        zx.append(remote(cb.at[pl.ds(to, zrows)], zx_buf.at[i], zx_s.at[i], zx_r.at[i], (samp_of(q, 0, 0), var)))

    xo = x_all[pl.ds(0, rows)]
    xf = xo.astype(F32)
    resid = dot(oh, xo)
    q = jnp.sum(xf * xf, axis=0, keepdims=True)
    q = q + jnp.sum(d_own * (2.0 * resid + count * d_own), axis=0, keepdims=True)
    q_src[...] = jnp.concatenate([q[:, j * 128 : (j + 1) * 128] for j in range(k // 128)] * 2, axis=0)
    qy = [
        remote(q_src, q_yc.at[i], qy_s.at[i], qy_r.at[i], (samp_of(0, *a), var)) for i, a in enumerate(YC)
    ]
    for cp in qy:
        cp.wait_recv()
    q2 = q_src[...]
    for i in range(len(YC)):
        q2 = q2 + q_yc[i]
    q2_src[...] = q2
    qz = [
        remote(q2_src, q_z.at[i], qz_s.at[i], qz_r.at[i], (samp_of(a, 0, 0), var)) for i, a in enumerate(ZD)
    ]

    for cp in zx:
        cp.wait_recv()
    acc = cross[pl.ds(pl.multiple_of(z * zrows, zrows), zrows)]
    for i in range(len(ZD)):
        acc = acc + zx_buf[i].astype(F32)
    for j in range(NY * NC):
        ysrc[j] = acc[j * 8 : (j + 1) * 8]
    yx = []
    for i, (dy, dc) in enumerate(YC):
        to = ((y + dy) % NY) * 2 + (c + dc) % NC
        yx.append(remote(ysrc.at[to], yx_buf.at[i], yx_s.at[i], yx_r.at[i], (samp_of(0, dy, dc), var)))
    for cp in qz:
        cp.wait_recv()
    q3 = q2
    for i in range(len(ZD)):
        q3 = q3 + q_z[i]
    spread = lax.rsqrt(q3[:4] / total + 1e-6) / total
    spread = jnp.concatenate([spread[j : j + 1] for j in range(4)], axis=1)
    at_row = lax.broadcasted_iota(jnp.int32, (8, k), 1) - samp * 8 == lax.broadcasted_iota(jnp.int32, (8, k), 0)
    scale = jnp.sum(jnp.where(at_row, spread, 0.0), axis=1, keepdims=True)

    for cp in yx:
        cp.wait_recv()
    same = ysrc[y * 2 + c]
    cross_half = jnp.zeros_like(same)
    for i, (dy, dc) in enumerate(YC):
        if dc:
            cross_half = cross_half + yx_buf[i]
        else:
            same = same + yx_buf[i]
    o_ref[:, pl.ds(mine, half)] = same * scale
    o_ref[:, pl.ds(other, half)] = cross_half * scale

    for cp in [cp_e2, cp_co2] + st + rs + ycs + ag + sb + zs + dms + zx + qy + qz + yx:
        cp.wait_send()


def shards(total, dosages, weights, prior, cohort, expression):
    rows, depth = dosages.shape
    k = weights.shape[1]
    genes = expression.shape[1]
    half = genes // 2
    width = prior.shape[1]
    blk = rows // 8
    out_rows = k // 64
    vm, sem = pltpu.VMEM, pltpu.SemaphoreType.DMA
    scratch = [
        vm((rows, depth), BF16), vm((depth, k), BF16), vm((width, rows), F32), vm((2, 1, rows), jnp.int32),
        vm((2 * rows, half), BF16), vm((3 * width + 4 * COHORTS, rows), BF16), vm((3 * width + 4 * COHORTS, k), BF16),
        vm((rows, k), BF16), vm((2 * blk, k), F32), vm((7, blk, k), BF16), vm((2 * rows, k), BF16),
        vm((8, COHORTS, 128), F32), vm((7, COHORTS, 128), F32), vm((COHORTS, 128), F32), vm((7, COHORTS, 128), F32),
        vm((COHORTS, 128), F32), vm((7, COHORTS, 128), F32),
        vm((COHORTS, 128), F32), vm((2, 8, COHORTS, 128), F32), vm((k, half), F32), vm((k, half), BF16),
        vm((7, k // 8, half), BF16), vm((8, out_rows, half), F32), vm((7, out_rows, half), F32),
        vm((8, 128), F32), vm((7, 8, 128), F32), vm((8, 128), F32), vm((7, 8, 128), F32),
        sem((5,)), sem((4,)), sem((7,)), sem((7,)), sem((7,)), sem((7,)), sem((7,)), sem((7,)),
        sem((15,)), sem((15,)), sem((7,)), sem((7,)), sem((7,)), sem((7,)), sem((8,)), sem((8,)),
        sem((7,)), sem((7,)), sem((7,)), sem((7,)), sem((7,)), sem((7,)), sem((7,)), sem((7,)),
    ]
    return pl.pallas_call(
        functools.partial(kernel, float(total)),
        out_shape=jax.ShapeDtypeStruct((out_rows, genes), F32),
        in_specs=[pl.BlockSpec(memory_space=pl.ANY)] * 5,
        out_specs=pl.BlockSpec(memory_space=pltpu.VMEM),
        scratch_shapes=scratch,
        compiler_params=pltpu.CompilerParams(
            collective_id=0, has_side_effects=True, vmem_limit_bytes=48 << 20
        ),
    )(dosages, weights, prior.T, cohort.reshape(1, rows), expression)


def solution(mesh):
    placed = (P("samp", "var"), P("var", None), P("samp", "var"), P("samp", None), P("samp", "var"))

    def run(dosages, weights, prior, cohort, expression):
        body = functools.partial(shards, dosages.shape[0])
        return jax.shard_map(body, mesh=mesh, in_specs=placed, out_specs=P("samp", "var"), check_vma=False)(
            dosages, weights, prior, cohort, expression
        )

    return run
```

time: 133 us -> 69 us (0.52)
  blocking collectives: 104 us -> 0 us
  Pallas kernels: 0 us -> 62.3 us
  waiting for transfers between devices: 11 us -> 0 us
  starting transfers between devices: 5.85 us -> 0 us
  other arithmetic: 4.21 us -> 0 us
  matrix products: 4.01 us -> 0 us
  local copies, waits for them, and re-layouts: 3.64 us -> 6.52 us
    all_to_all x4 -> x0, blocking collectives: 104 us -> none  [the longest x1 44.1 us: summed_on_arrival_2(): lax.all_to_all(parts, axis, split_axis=0, concat_axis=0, tiled=True)]
    pallas_call x0 -> x1, Pallas kernels: none -> 62.3 us  [shards(): pl.pallas_call(functools.partial(kernel, float(total)), out_shape=jax.Sha...]
    all_to_all x1 -> x0, waiting for transfers between devices: 11 us -> none  [summed_on_arrival(): lax.all_to_all(parts, axis, split_axis=0, concat_axis=0, tiled=True)]
    all_to_all x1 -> x0, starting transfers between devices: 5.85 us -> none  [summed_on_arrival(): lax.all_to_all(parts, axis, split_axis=0, concat_axis=0, tiled=True)]
    unnamed x10 -> x11, local copies, waits for them, and re-layouts: 2.5 us -> 6.52 us
    dot_general x4 -> x0, matrix products: 4.01 us -> none  [the longest x1 2.69 us: shards(): jnp.dot(dosages, weights, preferred_element_type=jnp.float32)]
    reduce_sum x7 -> x0, other arithmetic: 1.38 us -> none  [the longest x1 0.68 us: standardize(): total = jnp.sum(counts)]
  transfers between devices with their start and end apart: 1 -> 0, of which waited for: 1 -> 0; matrix products, arithmetic and copies ran while one was open for 0% -> 0% of each run, Pallas kernels for 0% -> 0%
where the time goes in v1:
time: 69 us; the launch traced here: 68.8 us
  Pallas kernels  62.3 us (90%)
  local copies, waits for them, and re-layouts  6.52 us (9%)
    pallas_call x1, Pallas kernels, shards(): pl.pallas_call(functools.partial(kernel, float(total)), out_shape=jax.Sha...  62.3 us
    unnamed x11, local copies, waits for them, and re-layouts  6.52 us

profile of v1, /device:TPU:1, one launch (start us, length us, event | category | flops | bytes accessed | tf_op | source)
XLA Modules:
  0.0 68.8 jit_solution(3572156014230307144)
XLA Ops:
  0.0 0.0 copy-start
  0.0 1.5 %copy-done = bf16[512,1792]{1,0:T(8,128)(2,1)S(1)} copy-done((bf16[512,1792]{1,0:T(8,128)(2,1)S(1)}, bf16[512,1792]{1,0:T(8,128)(2,1)}, u32[]{:S(2)}) %copy-start) | copy-done | bytes 1835032
  1.5 0.0 copy-start.1
  1.5 1.5 %copy-done.1 = bf16[1792,512]{1,0:T(8,128)(2,1)S(1)} copy-done((bf16[1792,512]{1,0:T(8,128)(2,1)S(1)}, bf16[1792,512]{1,0:T(8,128)(2,1)}, u32[]{:S(2)}) %copy-start.1) | copy-done | bytes 1835032
  3.0 0.0 copy-start.2
  3.0 1.3 %copy-done.2 = bf16[512,1280]{1,0:T(8,128)(2,1)S(1)} copy-done((bf16[512,1280]{1,0:T(8,128)(2,1)S(1)}, bf16[512,1280]{1,0:T(8,128)(2,1)}, u32[]{:S(2)}) %copy-start.2) | copy-done | bytes 1310744
  4.3 0.0 copy-start.3
  4.3 0.9 %copy-done.3 = f32[512,64]{0,1:T(8,128)S(1)} copy-done((f32[512,64]{0,1:T(8,128)S(1)}, f32[512,64]{0,1:T(8,128)}, u32[]{:S(2)}) %copy-start.3) | copy-done | bytes 131096
  5.2 0.0 copy-start.4
  5.2 0.7 copy-done.4
  5.9 62.3 %shard_map.55 = f32[8,1280]{1,0:T(8,128)S(1)} custom-call(bf16[512,1792]{1,0:T(8,128)(2,1)S(1)} %copy-done, bf16[1792,512]{1,0:T(8,128)(2,1)S(1)} %copy-done.1, f32[64,512]{1,0:T(8,128)S(1)} %bitcast.2, s32[1,512]{1,0:T(1,128)S(1)} %bitcast.3, bf16[512,1280]{1,0:T(8,128)(2,1)S(1)} %copy-done.2), custom_call_target="tpu_custom_call" | custom-call | tf_op jit(solution)/shard_map/pallas_call | solution.py:329
  68.2 0.6 copy.7
Async XLA Ops:
  0.0 1.5 %copy-start = (bf16[512,1792]{1,0:T(8,128)(2,1)S(1)}, bf16[512,1792]{1,0:T(8,128)(2,1)}, u32[]{:S(2)}) copy-start(bf16[512,1792]{1,0:T(8,128)(2,1)} %d_hbm.1) | copy-start | bytes 5505028
  1.5 1.5 %copy-start.1 = (bf16[1792,512]{1,0:T(8,128)(2,1)S(1)}, bf16[1792,512]{1,0:T(8,128)(2,1)}, u32[]{:S(2)}) copy-start(bf16[1792,512]{1,0:T(8,128)(2,1)} %w_hbm.1) | copy-start | bytes 5505028
  3.0 1.3 %copy-start.2 = (bf16[512,1280]{1,0:T(8,128)(2,1)S(1)}, bf16[512,1280]{1,0:T(8,128)(2,1)}, u32[]{:S(2)}) copy-start(bf16[512,1280]{1,0:T(8,128)(2,1)} %e_hbm.1) | copy-start | bytes 3932164
  4.3 0.9 %copy-start.3 = (f32[512,64]{0,1:T(8,128)S(1)}, f32[512,64]{0,1:T(8,128)}, u32[]{:S(2)}) copy-start(f32[512,64]{0,1:T(8,128)} %param.7) | copy-start | bytes 393220
  5.2 0.7 copy-start.4

commit v2 on v1

--- a/solution.py
+++ b/solution.py
@@ -15,6 +15,11 @@
 VAR = [(dx, dl) for dx in (2, 1, 3, 0) for dl in (1, 0) if dx or dl]
 YC = [(dy, dc) for dy in (2, 1, 3, 0) for dc in (1, 0) if dy or dc]
 ZD = [4, 3, 5, 2, 6, 1, 7]
+DY = (2, 1, 3, 0)
+
+
+def hops_of(chunk, way):
+    return 4 if (chunk + way) % 2 == 0 else 3
 
 
 def split2(a):
@@ -44,7 +49,7 @@
 def kernel(
     total, d_hbm, w_hbm, p_hbm, co_hbm, e_hbm, o_ref,
     d, w, p, co, e_all, lt, rt, snd, own, rs_buf, x_all, st_src, st_buf, t_src, yc_buf, t2_src, z_buf,
-    d_src, dm, cross, cb, zx_buf, ysrc, yx_buf, q_src, q_yc, q2_src, q_z,
+    d_src, dm, cross, cb, zx_buf, zx_src, ysrc, yx_buf, q_src, q_yc, q2_src, q_z,
     ld, e_sem, st_s, st_r, yc_s, yc_r, z_s, z_r, dm_s, dm_r, rs_s, rs_r, ag_s, ag_r, sb_s, sb_r,
     zx_s, zx_r, yx_s, yx_r, qy_s, qy_r, qz_s, qz_r,
 ):
@@ -89,12 +94,11 @@
         pl.semaphore_signal(barrier, inc=1, device_id=dev, device_id_type=MESH)
 
     cp_co = local(co_hbm, co.at[0], ld.at[0])
+    cp_p = local(p_hbm, p, ld.at[3])
     cp_d = local(d_hbm, d, ld.at[1])
     cp_w = local(w_hbm, w, ld.at[2])
-    cp_p = local(p_hbm, p, ld.at[3])
     mine = pl.multiple_of(c * half, 128)
     other = pl.multiple_of((1 - c) * half, 128)
-    cp_e = local(e_hbm.at[:, pl.ds(mine, half)], e_all.at[pl.ds(0, rows)], ld.at[4])
 
     cp_co.wait()
     cohorts = lax.broadcasted_iota(jnp.int32, (COHORTS, rows), 0)
@@ -130,13 +134,14 @@
         st_src[2 * j + 1] = jnp.where(low, pltpu.roll(pair, 64, 1), count)
 
     pl.semaphore_wait(barrier, len(peers))
-    cp_e2 = remote(e_hbm.at[:, pl.ds(other, half)], e_all.at[pl.ds(rows, rows)], e_sem.at[0], e_sem.at[1], sib)
-    cp_co2 = remote(co_hbm, co.at[1], e_sem.at[2], e_sem.at[3], sib)
     st = [
         remote(st_src.at[var_of(*q)], st_buf.at[i], st_s.at[i], st_r.at[i], (samp, var_of(*q)))
         for i, q in enumerate(VAR)
     ]
 
+    cp_e2 = remote(e_hbm.at[:, pl.ds(other, half)], e_all.at[pl.ds(rows, rows)], e_sem.at[0], e_sem.at[1], sib)
+    cp_co2 = remote(co_hbm, co.at[1], e_sem.at[2], e_sem.at[3], sib)
+    cp_e = local(e_hbm.at[:, pl.ds(mine, half)], e_all.at[pl.ds(0, rows)], ld.at[4])
     rs = []
     for step, dx in enumerate((2, 1, 3, 0)):
         xo = (x + dx) % NX
@@ -243,10 +248,21 @@
     full = cross[...] + dot_t(left, right)
     cross[...] = full
     cb[...] = full.astype(BF16)
-    zx = []
-    for i, q in enumerate(ZD):
-        to = pl.multiple_of(((z + q) % NZ) * zrows, zrows)
-        zx.append(remote(cb.at[pl.ds(to, zrows)], zx_buf.at[i], zx_s.at[i], zx_r.at[i], (samp_of(q, 0, 0), var)))
+    sub = zrows // NY
+
+    def chunk_rows(dest, dy):
+        return pl.ds(pl.multiple_of((dest % NZ) * zrows + ((y + dy) % NY) * sub, sub), sub)
+
+    def hop(i, a, t, src):
+        return remote(
+            src, zx_buf.at[i, a, t], zx_s.at[i, a, t], zx_r.at[i, a, t], (samp_of(1 - 2 * a, 0, 0), var)
+        )
+
+    ring = {}
+    for i, dy in enumerate(DY):
+        for a in range(2):
+            n = hops_of(i, a)
+            ring[i, a, 0] = hop(i, a, 0, cb.at[chunk_rows(z + (1 - 2 * a) * n + NZ, dy)])
 
     xo = x_all[pl.ds(0, rows)]
     xf = xo.astype(F32)
@@ -257,27 +273,44 @@
     qy = [
         remote(q_src, q_yc.at[i], qy_s.at[i], qy_r.at[i], (samp_of(0, *a), var)) for i, a in enumerate(YC)
     ]
-    for cp in qy:
-        cp.wait_recv()
-    q2 = q_src[...]
-    for i in range(len(YC)):
-        q2 = q2 + q_yc[i]
-    q2_src[...] = q2
-    qz = [
-        remote(q2_src, q_z.at[i], qz_s.at[i], qz_r.at[i], (samp_of(a, 0, 0), var)) for i, a in enumerate(ZD)
-    ]
-
-    for cp in zx:
-        cp.wait_recv()
-    acc = cross[pl.ds(pl.multiple_of(z * zrows, zrows), zrows)]
-    for i in range(len(ZD)):
-        acc = acc + zx_buf[i].astype(F32)
-    for j in range(NY * NC):
-        ysrc[j] = acc[j * 8 : (j + 1) * 8]
-    yx = []
-    for i, (dy, dc) in enumerate(YC):
-        to = ((y + dy) % NY) * 2 + (c + dc) % NC
-        yx.append(remote(ysrc.at[to], yx_buf.at[i], yx_s.at[i], yx_r.at[i], (samp_of(0, dy, dc), var)))
+    yx = {}
+    for t in range(1, 5):
+        if t == 3:
+            for cp in qy:
+                cp.wait_recv()
+            q2 = q_src[...]
+            for i in range(len(YC)):
+                q2 = q2 + q_yc[i]
+            q2_src[...] = q2
+            qz = [
+                remote(q2_src, q_z.at[i], qz_s.at[i], qz_r.at[i], (samp_of(b, 0, 0), var))
+                for i, b in enumerate(ZD)
+            ]
+        for i, dy in enumerate(DY):
+            for a in range(2):
+                n = hops_of(i, a)
+                if t >= n:
+                    continue
+                ring[i, a, t - 1].wait_recv()
+                part = zx_buf[i, a, t - 1].astype(F32) + cross[chunk_rows(z + (1 - 2 * a) * (n - t) + NZ, dy)]
+                zx_src[i, a, t] = part.astype(BF16)
+                ring[i, a, t] = hop(i, a, t, zx_src.at[i, a, t])
+            if t == 4:
+                acc = cross[chunk_rows(z, dy)]
+                for a in range(2):
+                    n = hops_of(i, a)
+                    ring[i, a, n - 1].wait_recv()
+                    acc = acc + zx_buf[i, a, n - 1].astype(F32)
+                ysrc[i, 0] = acc[:8]
+                ysrc[i, 1] = acc[8:]
+                for dc in (1, 0):
+                    if dy or dc:
+                        m = YC.index((dy, dc))
+                        yx[m] = remote(
+                            ysrc.at[i, (c + dc) % NC], yx_buf.at[m], yx_s.at[m], yx_r.at[m], (samp_of(0, dy, dc), var)
+                        )
+    yx = [yx[m] for m in range(len(YC))]
+    zx = list(ring.values())
     for cp in qz:
         cp.wait_recv()
     q3 = q2
@@ -290,7 +323,7 @@
 
     for cp in yx:
         cp.wait_recv()
-    same = ysrc[y * 2 + c]
+    same = ysrc[len(DY) - 1, c]
     cross_half = jnp.zeros_like(same)
     for i, (dy, dc) in enumerate(YC):
         if dc:
@@ -320,11 +353,11 @@
         vm((8, COHORTS, 128), F32), vm((7, COHORTS, 128), F32), vm((COHORTS, 128), F32), vm((7, COHORTS, 128), F32),
         vm((COHORTS, 128), F32), vm((7, COHORTS, 128), F32),
         vm((COHORTS, 128), F32), vm((2, 8, COHORTS, 128), F32), vm((k, half), F32), vm((k, half), BF16),
-        vm((7, k // 8, half), BF16), vm((8, out_rows, half), F32), vm((7, out_rows, half), F32),
+        vm((4, 2, 4, k // 32, half), BF16), vm((4, 2, 4, k // 32, half), BF16), vm((4, 2, out_rows, half), F32), vm((7, out_rows, half), F32),
         vm((8, 128), F32), vm((7, 8, 128), F32), vm((8, 128), F32), vm((7, 8, 128), F32),
         sem((5,)), sem((4,)), sem((7,)), sem((7,)), sem((7,)), sem((7,)), sem((7,)), sem((7,)),
         sem((15,)), sem((15,)), sem((7,)), sem((7,)), sem((7,)), sem((7,)), sem((8,)), sem((8,)),
-        sem((7,)), sem((7,)), sem((7,)), sem((7,)), sem((7,)), sem((7,)), sem((7,)), sem((7,)),
+        sem((4, 2, 4)), sem((4, 2, 4)), sem((7,)), sem((7,)), sem((7,)), sem((7,)), sem((7,)), sem((7,)),
     ]
     return pl.pallas_call(
         functools.partial(kernel, float(total)),
@@ -333,7 +366,7 @@
         out_specs=pl.BlockSpec(memory_space=pltpu.VMEM),
         scratch_shapes=scratch,
         compiler_params=pltpu.CompilerParams(
-            collective_id=0, has_side_effects=True, vmem_limit_bytes=48 << 20
+            collective_id=0, has_side_effects=True, vmem_limit_bytes=67043328
         ),
     )(dosages, weights, prior.T, cohort.reshape(1, rows), expression)
 

time: 69 us -> 60.7 us (0.88)
  local copies, waits for them, and re-layouts: 6.52 us -> 1.4 us
  Pallas kernels: 62.3 us -> 59.1 us
    unnamed x11 -> x1, local copies, waits for them, and re-layouts: 6.52 us -> 1.4 us
    pallas_call x1, Pallas kernels: 62.3 us -> 59.1 us  [shards(): pl.pallas_call(functools.partial(kernel, float(total)), out_shape=jax.Sha...]
where the time goes in v2:
time: 60.7 us; the launch traced here: 60.5 us
  Pallas kernels  59.1 us (97%)
  local copies, waits for them, and re-layouts  1.4 us (2%)
    pallas_call x1, Pallas kernels, shards(): pl.pallas_call(functools.partial(kernel, float(total)), out_shape=jax.Sha...  59.1 us
    unnamed x1, local copies, waits for them, and re-layouts  1.4 us

profile of v2, /device:TPU:1, one launch (start us, length us, event | category | flops | bytes accessed | tf_op | source)
XLA Modules:
  0.0 60.5 jit_solution(5712554873682067439)
XLA Ops:
  0.0 59.1 %shard_map.55 = f32[8,1280]{1,0:T(8,128)} custom-call(bf16[512,1792]{1,0:T(8,128)(2,1)} %d_hbm.1, bf16[1792,512]{1,0:T(8,128)(2,1)} %w_hbm.1, f32[64,512]{1,0:T(8,128)} %bitcast.2, s32[1,512]{1,0:T(1,128)} %bitcast.3, bf16[512,1280]{1,0:T(8,128)(2,1)} %e_hbm.1), custom_call_target="tpu_custom_call" | custom-call | tf_op jit(solution)/shard_map/pallas_call | solution.py:362
  59.1 1.4 %copy.7 = f32[8,1280]{1,0:T(8,128)} copy(f32[8,1280]{1,0:T(8,128)} %shard_map.55) | data formatting | bytes 81920

commit v3 on v1

--- a/solution.py
+++ b/solution.py
@@ -15,6 +15,7 @@
 VAR = [(dx, dl) for dx in (2, 1, 3, 0) for dl in (1, 0) if dx or dl]
 YC = [(dy, dc) for dy in (2, 1, 3, 0) for dc in (1, 0) if dy or dc]
 ZD = [4, 3, 5, 2, 6, 1, 7]
+DY = (2, 1, 3, 0)
 
 
 def split2(a):
@@ -44,7 +45,7 @@
 def kernel(
     total, d_hbm, w_hbm, p_hbm, co_hbm, e_hbm, o_ref,
     d, w, p, co, e_all, lt, rt, snd, own, rs_buf, x_all, st_src, st_buf, t_src, yc_buf, t2_src, z_buf,
-    d_src, dm, cross, cb, zx_buf, ysrc, yx_buf, q_src, q_yc, q2_src, q_z,
+    d_src, dm, cross, cb, zx_buf, zx_src, ysrc, yx_buf, q_src, q_yc, q2_src, q_z,
     ld, e_sem, st_s, st_r, yc_s, yc_r, z_s, z_r, dm_s, dm_r, rs_s, rs_r, ag_s, ag_r, sb_s, sb_r,
     zx_s, zx_r, yx_s, yx_r, qy_s, qy_r, qz_s, qz_r,
 ):
@@ -89,12 +90,11 @@
         pl.semaphore_signal(barrier, inc=1, device_id=dev, device_id_type=MESH)
 
     cp_co = local(co_hbm, co.at[0], ld.at[0])
+    cp_p = local(p_hbm, p, ld.at[3])
     cp_d = local(d_hbm, d, ld.at[1])
     cp_w = local(w_hbm, w, ld.at[2])
-    cp_p = local(p_hbm, p, ld.at[3])
     mine = pl.multiple_of(c * half, 128)
     other = pl.multiple_of((1 - c) * half, 128)
-    cp_e = local(e_hbm.at[:, pl.ds(mine, half)], e_all.at[pl.ds(0, rows)], ld.at[4])
 
     cp_co.wait()
     cohorts = lax.broadcasted_iota(jnp.int32, (COHORTS, rows), 0)
@@ -130,31 +130,36 @@
         st_src[2 * j + 1] = jnp.where(low, pltpu.roll(pair, 64, 1), count)
 
     pl.semaphore_wait(barrier, len(peers))
-    cp_e2 = remote(e_hbm.at[:, pl.ds(other, half)], e_all.at[pl.ds(rows, rows)], e_sem.at[0], e_sem.at[1], sib)
-    cp_co2 = remote(co_hbm, co.at[1], e_sem.at[2], e_sem.at[3], sib)
     st = [
         remote(st_src.at[var_of(*q)], st_buf.at[i], st_s.at[i], st_r.at[i], (samp, var_of(*q)))
         for i, q in enumerate(VAR)
     ]
 
-    rs = []
-    for step, dx in enumerate((2, 1, 3, 0)):
+    cp_e2 = remote(e_hbm.at[:, pl.ds(other, half)], e_all.at[pl.ds(rows, rows)], e_sem.at[0], e_sem.at[1], sib)
+    cp_co2 = remote(co_hbm, co.at[1], e_sem.at[2], e_sem.at[3], sib)
+    cp_e = local(e_hbm.at[:, pl.ds(mine, half)], e_all.at[pl.ds(0, rows)], ld.at[4])
+    hb = blk // 2
+
+    def send_part(q, h):
+        i = VAR.index(q)
+        to = var_of(*q)
+        return remote(
+            snd.at[pl.ds(pl.multiple_of(to * blk + h * hb, hb), hb)], rs_buf.at[i, h], rs_s.at[i, h], rs_r.at[i, h], (samp, to)
+        )
+
+    rs = {}
+    for dx in (2, 1, 3, 0):
         xo = (x + dx) % NX
         r0 = pl.multiple_of(xo * (2 * blk), 2 * blk)
         f = dot(d[pl.ds(r0, 2 * blk)], w[...]) + dot_t(lt[:, pl.ds(r0, 2 * blk)], rt[...])
         snd[pl.ds(r0, 2 * blk)] = f.astype(BF16)
         if dx == 0:
             own[...] = f
-        for dl in (1, 0):
-            if dx or dl:
-                i = VAR.index((dx, dl))
-                to = var_of(dx, dl)
-                rs.append(
-                    remote(
-                        snd.at[pl.ds(pl.multiple_of(to * blk, blk), blk)], rs_buf.at[i], rs_s.at[i], rs_r.at[i],
-                        (samp, to),
-                    )
-                )
+        for q in VAR:
+            if q[0] == dx:
+                rs[q, 0] = send_part(q, 0)
+    for q in VAR:
+        rs[q, 1] = send_part(q, 1)
 
     for cp in st:
         cp.wait_recv()
@@ -163,8 +168,8 @@
         t = t + st_buf[i]
     t = jnp.where(low, t, count)
     t_src[...] = t
-    ycs = [
-        remote(t_src, yc_buf.at[i], yc_s.at[i], yc_r.at[i], (samp_of(0, *q), var)) for i, q in enumerate(YC)
+    zs = [
+        remote(t_src, z_buf.at[i], z_s.at[i], z_r.at[i], (samp_of(q, 0, 0), var)) for i, q in enumerate(ZD)
     ]
     cp_e.wait()
     e_own = dot(oh, e_all[pl.ds(0, rows)])
@@ -173,45 +178,51 @@
     oh2 = (co[1] == cohorts).astype(F32).astype(BF16)
     e_sib = dot(oh2, e_all[pl.ds(rows, rows)])
 
-    for cp in rs:
-        cp.wait_recv()
-    at = pl.multiple_of(l * blk, blk)
-    s = own[pl.ds(at, blk)]
-    for i in range(len(VAR)):
-        s = s + rs_buf[i].astype(F32)
-    row = pl.multiple_of(var * blk, blk)
-    x_all[pl.ds(row, blk)] = s.astype(BF16)
-    ag = [
-        remote(x_all.at[pl.ds(row, blk)], x_all.at[pl.ds(row, blk)], ag_s.at[i], ag_r.at[i], (samp, var_of(*q)))
-        for i, q in enumerate(VAR)
-    ]
-    sb = [
-        remote(x_all.at[pl.ds(row, blk)], x_all.at[pl.ds(pl.multiple_of(rows + row, blk), blk)], sb_s.at[7], sb_r.at[7], sib)
-    ]
-
+    ag, sb = {}, {}
+
+    def spread_part(h):
+        for q in VAR:
+            rs[q, h].wait_recv()
+        s = own[pl.ds(pl.multiple_of(l * blk + h * hb, hb), hb)]
+        for i in range(len(VAR)):
+            s = s + rs_buf[i, h].astype(F32)
+        row = pl.multiple_of(var * blk + h * hb, hb)
+        x_all[pl.ds(row, hb)] = s.astype(BF16)
+        for i, q in enumerate(VAR):
+            ag[i, h] = remote(
+                x_all.at[pl.ds(row, hb)], x_all.at[pl.ds(row, hb)], ag_s.at[i, h], ag_r.at[i, h], (samp, var_of(*q))
+            )
+        sb[7, h] = share(7, h, row)
+
+    def share(i, h, row):
+        return remote(
+            x_all.at[pl.ds(row, hb)], x_all.at[pl.ds(pl.multiple_of(rows + row, hb), hb)], sb_s.at[i, h], sb_r.at[i, h], sib
+        )
+
+    spread_part(0)
+    for cp in zs:
+        cp.wait_recv()
+    t2 = t
+    for i in range(len(ZD)):
+        t2 = t2 + z_buf[i]
+    t2_src[...] = t2
+    ycs = [
+        remote(t2_src, yc_buf.at[i], yc_s.at[i], yc_r.at[i], (samp_of(0, *q), var)) for i, q in enumerate(YC)
+    ]
+    spread_part(1)
+
+    def pass_on(h):
+        for i in range(len(VAR) - 1, -1, -1):
+            dx, dl = VAR[i]
+            ag[i, h].wait_recv()
+            sb[i, h] = share(i, h, pl.multiple_of(var_of(-dx, -dl) * blk + h * hb, hb))
+
+    pass_on(0)
     for cp in ycs:
         cp.wait_recv()
-    t2 = t
+    t3 = t2
     for i in range(len(YC)):
-        t2 = t2 + yc_buf[i]
-    t2_src[...] = t2
-    zs = [
-        remote(t2_src, z_buf.at[i], z_s.at[i], z_r.at[i], (samp_of(q, 0, 0), var)) for i, q in enumerate(ZD)
-    ]
-    for i in range(len(VAR) - 1, -1, -1):
-        dx, dl = VAR[i]
-        ag[i].wait_recv()
-        got = pl.multiple_of(var_of(-dx, -dl) * blk, blk)
-        sb.append(
-            remote(
-                x_all.at[pl.ds(got, blk)], x_all.at[pl.ds(pl.multiple_of(rows + got, blk), blk)], sb_s.at[i], sb_r.at[i], sib
-            )
-        )
-    for cp in zs:
-        cp.wait_recv()
-    t3 = t2
-    for i in range(len(ZD)):
-        t3 = t3 + z_buf[i]
+        t3 = t3 + yc_buf[i]
     mean = t3 / pltpu.roll(t3, 64, 1)
     d_src[...] = jnp.where(low, t / jnp.maximum(count, 1.0) - mean, 0.0)
     dm[0, var] = d_src[...]
@@ -224,7 +235,8 @@
             )
     dms.append(remote(d_src, dm.at[1, var], dm_s.at[14], dm_r.at[14], sib))
 
-    for cp in sb:
+    pass_on(1)
+    for cp in sb.values():
         cp.wait_recv()
     cross[...] = dot_t(x_all[...], e_all[...])
     for cp in dms:
@@ -243,10 +255,25 @@
     full = cross[...] + dot_t(left, right)
     cross[...] = full
     cb[...] = full.astype(BF16)
-    zx = []
-    for i, q in enumerate(ZD):
-        to = pl.multiple_of(((z + q) % NZ) * zrows, zrows)
-        zx.append(remote(cb.at[pl.ds(to, zrows)], zx_buf.at[i], zx_s.at[i], zx_r.at[i], (samp_of(q, 0, 0), var)))
+    sub = zrows // NY
+
+    def chunk_rows(dest, dy):
+        return pl.ds(pl.multiple_of((dest % NZ) * zrows + ((y + dy) % NY) * sub, sub), sub)
+
+    def hop(i, n, to, src):
+        return remote(
+            src, zx_buf.at[i, n], zx_s.at[i, n], zx_r.at[i, n], (samp_of(to, 0, 0), var)
+        )
+
+    zx = {}
+    for i, dy in enumerate(DY):
+        turn = 1 if i % 2 == 0 else -1
+        zx[i, 0] = hop(i, 0, 2 * turn, cb.at[chunk_rows(z + 4, dy)])
+        zx[i, 1] = hop(i, 1, 1, cb.at[chunk_rows(z + 3, dy)])
+        zx[i, 2] = hop(i, 2, -1, cb.at[chunk_rows(z + NZ - 3, dy)])
+    for i, dy in enumerate(DY):
+        zx[i, 5] = hop(i, 5, 1, cb.at[chunk_rows(z + 1, dy)])
+        zx[i, 6] = hop(i, 6, -1, cb.at[chunk_rows(z + NZ - 1, dy)])
 
     xo = x_all[pl.ds(0, rows)]
     xf = xo.astype(F32)
@@ -257,6 +284,16 @@
     qy = [
         remote(q_src, q_yc.at[i], qy_s.at[i], qy_r.at[i], (samp_of(0, *a), var)) for i, a in enumerate(YC)
     ]
+    for i, dy in enumerate(DY):
+        turn = 1 if i % 2 == 0 else -1
+        for n in range(3):
+            zx[i, n].wait_recv()
+        for a, way in enumerate((1, -1)):
+            part = cross[chunk_rows(z + 2 * way + NZ, dy)] + zx_buf[i, 1 + a].astype(F32)
+            if way == turn:
+                part = part + zx_buf[i, 0].astype(F32)
+            zx_src[i, a] = part.astype(BF16)
+            zx[i, 3 + a] = hop(i, 3 + a, 2 * way, zx_src.at[i, a])
     for cp in qy:
         cp.wait_recv()
     q2 = q_src[...]
@@ -264,20 +301,24 @@
         q2 = q2 + q_yc[i]
     q2_src[...] = q2
     qz = [
-        remote(q2_src, q_z.at[i], qz_s.at[i], qz_r.at[i], (samp_of(a, 0, 0), var)) for i, a in enumerate(ZD)
-    ]
-
-    for cp in zx:
-        cp.wait_recv()
-    acc = cross[pl.ds(pl.multiple_of(z * zrows, zrows), zrows)]
-    for i in range(len(ZD)):
-        acc = acc + zx_buf[i].astype(F32)
-    for j in range(NY * NC):
-        ysrc[j] = acc[j * 8 : (j + 1) * 8]
-    yx = []
-    for i, (dy, dc) in enumerate(YC):
-        to = ((y + dy) % NY) * 2 + (c + dc) % NC
-        yx.append(remote(ysrc.at[to], yx_buf.at[i], yx_s.at[i], yx_r.at[i], (samp_of(0, dy, dc), var)))
+        remote(q2_src, q_z.at[i], qz_s.at[i], qz_r.at[i], (samp_of(b, 0, 0), var)) for i, b in enumerate(ZD)
+    ]
+    yx = {}
+    for i, dy in enumerate(DY):
+        acc = cross[chunk_rows(z, dy)]
+        for n in (5, 6, 3, 4):
+            zx[i, n].wait_recv()
+            acc = acc + zx_buf[i, n].astype(F32)
+        ysrc[i, 0] = acc[:8]
+        ysrc[i, 1] = acc[8:]
+        for dc in (1, 0):
+            if dy or dc:
+                m = YC.index((dy, dc))
+                yx[m] = remote(
+                    ysrc.at[i, (c + dc) % NC], yx_buf.at[m], yx_s.at[m], yx_r.at[m], (samp_of(0, dy, dc), var)
+                )
+    yx = [yx[m] for m in range(len(YC))]
+    zx, rs, ag, sb = [list(group.values()) for group in (zx, rs, ag, sb)]
     for cp in qz:
         cp.wait_recv()
     q3 = q2
@@ -290,7 +331,7 @@
 
     for cp in yx:
         cp.wait_recv()
-    same = ysrc[y * 2 + c]
+    same = ysrc[len(DY) - 1, c]
     cross_half = jnp.zeros_like(same)
     for i, (dy, dc) in enumerate(YC):
         if dc:
@@ -316,15 +357,15 @@
     scratch = [
         vm((rows, depth), BF16), vm((depth, k), BF16), vm((width, rows), F32), vm((2, 1, rows), jnp.int32),
         vm((2 * rows, half), BF16), vm((3 * width + 4 * COHORTS, rows), BF16), vm((3 * width + 4 * COHORTS, k), BF16),
-        vm((rows, k), BF16), vm((2 * blk, k), F32), vm((7, blk, k), BF16), vm((2 * rows, k), BF16),
+        vm((rows, k), BF16), vm((2 * blk, k), F32), vm((7, 2, blk // 2, k), BF16), vm((2 * rows, k), BF16),
         vm((8, COHORTS, 128), F32), vm((7, COHORTS, 128), F32), vm((COHORTS, 128), F32), vm((7, COHORTS, 128), F32),
         vm((COHORTS, 128), F32), vm((7, COHORTS, 128), F32),
         vm((COHORTS, 128), F32), vm((2, 8, COHORTS, 128), F32), vm((k, half), F32), vm((k, half), BF16),
-        vm((7, k // 8, half), BF16), vm((8, out_rows, half), F32), vm((7, out_rows, half), F32),
+        vm((4, 7, k // 32, half), BF16), vm((4, 2, k // 32, half), BF16), vm((4, 2, out_rows, half), F32), vm((7, out_rows, half), F32),
         vm((8, 128), F32), vm((7, 8, 128), F32), vm((8, 128), F32), vm((7, 8, 128), F32),
         sem((5,)), sem((4,)), sem((7,)), sem((7,)), sem((7,)), sem((7,)), sem((7,)), sem((7,)),
-        sem((15,)), sem((15,)), sem((7,)), sem((7,)), sem((7,)), sem((7,)), sem((8,)), sem((8,)),
-        sem((7,)), sem((7,)), sem((7,)), sem((7,)), sem((7,)), sem((7,)), sem((7,)), sem((7,)),
+        sem((15,)), sem((15,)), sem((7, 2)), sem((7, 2)), sem((7, 2)), sem((7, 2)), sem((8, 2)), sem((8, 2)),
+        sem((4, 7)), sem((4, 7)), sem((7,)), sem((7,)), sem((7,)), sem((7,)), sem((7,)), sem((7,)),
     ]
     return pl.pallas_call(
         functools.partial(kernel, float(total)),
@@ -333,7 +374,7 @@
         out_specs=pl.BlockSpec(memory_space=pltpu.VMEM),
         scratch_shapes=scratch,
         compiler_params=pltpu.CompilerParams(
-            collective_id=0, has_side_effects=True, vmem_limit_bytes=48 << 20
+            collective_id=0, has_side_effects=True, vmem_limit_bytes=67043328
         ),
     )(dosages, weights, prior.T, cohort.reshape(1, rows), expression)
 

time: 69 us -> 55.4 us (0.80)
  Pallas kernels: 62.3 us -> 53.8 us
  local copies, waits for them, and re-layouts: 6.52 us -> 1.4 us
    pallas_call x1, Pallas kernels: 62.3 us -> 53.8 us  [shards(): pl.pallas_call(functools.partial(kernel, float(total)), out_shape=jax.Sha...]
    unnamed x11 -> x1, local copies, waits for them, and re-layouts: 6.52 us -> 1.4 us
where the time goes in v3:
time: 55.4 us; the launch traced here: 55.2 us
  Pallas kernels  53.8 us (97%)
  local copies, waits for them, and re-layouts  1.4 us (3%)
    pallas_call x1, Pallas kernels, shards(): pl.pallas_call(functools.partial(kernel, float(total)), out_shape=jax.Sha...  53.8 us
    unnamed x1, local copies, waits for them, and re-layouts  1.4 us

profile of v3, /device:TPU:1, one launch (start us, length us, event | category | flops | bytes accessed | tf_op | source)
XLA Modules:
  0.0 55.2 jit_solution(6096903675568091143)
XLA Ops:
  0.0 53.8 %shard_map.55 = f32[8,1280]{1,0:T(8,128)} custom-call(bf16[512,1792]{1,0:T(8,128)(2,1)} %d_hbm.1, bf16[1792,512]{1,0:T(8,128)(2,1)} %w_hbm.1, f32[64,512]{1,0:T(8,128)} %bitcast.2, s32[1,512]{1,0:T(1,128)} %bitcast.3, bf16[512,1280]{1,0:T(8,128)(2,1)} %e_hbm.1), custom_call_target="tpu_custom_call" | custom-call | tf_op jit(solution)/shard_map/pallas_call | solution.py:370
  53.8 1.4 %copy.7 = f32[8,1280]{1,0:T(8,128)} copy(f32[8,1280]{1,0:T(8,128)} %shard_map.55) | data formatting | bytes 81920

commit v4 on v3

--- a/solution.py
+++ b/solution.py
@@ -45,7 +45,7 @@
 def kernel(
     total, d_hbm, w_hbm, p_hbm, co_hbm, e_hbm, o_ref,
     d, w, p, co, e_all, lt, rt, snd, own, rs_buf, x_all, st_src, st_buf, t_src, yc_buf, t2_src, z_buf,
-    d_src, dm, cross, cb, zx_buf, zx_src, ysrc, yx_buf, q_src, q_yc, q2_src, q_z,
+    d_src, dm, cross, cb, zx_buf, zx_src, own_y, ysrc, yx_buf, q_src, q_yc, q2_src, q_z,
     ld, e_sem, st_s, st_r, yc_s, yc_r, z_s, z_r, dm_s, dm_r, rs_s, rs_r, ag_s, ag_r, sb_s, sb_r,
     zx_s, zx_r, yx_s, yx_r, qy_s, qy_r, qz_s, qz_r,
 ):
@@ -139,28 +139,24 @@
     cp_co2 = remote(co_hbm, co.at[1], e_sem.at[2], e_sem.at[3], sib)
     cp_e = local(e_hbm.at[:, pl.ds(mine, half)], e_all.at[pl.ds(0, rows)], ld.at[4])
     hb = blk // 2
-
-    def send_part(q, h):
-        i = VAR.index(q)
-        to = var_of(*q)
-        return remote(
-            snd.at[pl.ds(pl.multiple_of(to * blk + h * hb, hb), hb)], rs_buf.at[i, h], rs_s.at[i, h], rs_r.at[i, h], (samp, to)
-        )
+    hr = rows // 2
+
+    def product(h):
+        f = dot(d[h * hr : (h + 1) * hr], w[...]) + dot_t(lt[:, h * hr : (h + 1) * hr], rt[...])
+        snd[h] = f.astype(BF16)
+        own[h] = f
+
+    def send_parts(h):
+        for i, q in enumerate(VAR):
+            to = var_of(*q)
+            rs[q, h] = remote(
+                snd.at[h, pl.ds(pl.multiple_of(to * hb, hb), hb)], rs_buf.at[i, h], rs_s.at[i, h], rs_r.at[i, h], (samp, to)
+            )
 
     rs = {}
-    for dx in (2, 1, 3, 0):
-        xo = (x + dx) % NX
-        r0 = pl.multiple_of(xo * (2 * blk), 2 * blk)
-        f = dot(d[pl.ds(r0, 2 * blk)], w[...]) + dot_t(lt[:, pl.ds(r0, 2 * blk)], rt[...])
-        snd[pl.ds(r0, 2 * blk)] = f.astype(BF16)
-        if dx == 0:
-            own[...] = f
-        for q in VAR:
-            if q[0] == dx:
-                rs[q, 0] = send_part(q, 0)
-    for q in VAR:
-        rs[q, 1] = send_part(q, 1)
-
+    product(0)
+    send_parts(0)
+    product(1)
     for cp in st:
         cp.wait_recv()
     t = st_src[var]
@@ -171,6 +167,7 @@
     zs = [
         remote(t_src, z_buf.at[i], z_s.at[i], z_r.at[i], (samp_of(q, 0, 0), var)) for i, q in enumerate(ZD)
     ]
+    send_parts(1)
     cp_e.wait()
     e_own = dot(oh, e_all[pl.ds(0, rows)])
     cp_e2.wait_recv()
@@ -183,10 +180,10 @@
     def spread_part(h):
         for q in VAR:
             rs[q, h].wait_recv()
-        s = own[pl.ds(pl.multiple_of(l * blk + h * hb, hb), hb)]
+        s = own[h, pl.ds(pl.multiple_of(var * hb, hb), hb)]
         for i in range(len(VAR)):
             s = s + rs_buf[i, h].astype(F32)
-        row = pl.multiple_of(var * blk + h * hb, hb)
+        row = pl.multiple_of(h * hr + var * hb, hb)
         x_all[pl.ds(row, hb)] = s.astype(BF16)
         for i, q in enumerate(VAR):
             ag[i, h] = remote(
@@ -215,7 +212,14 @@
         for i in range(len(VAR) - 1, -1, -1):
             dx, dl = VAR[i]
             ag[i, h].wait_recv()
-            sb[i, h] = share(i, h, pl.multiple_of(var_of(-dx, -dl) * blk + h * hb, hb))
+            sb[i, h] = share(i, h, pl.multiple_of(h * hr + var_of(-dx, -dl) * hb, hb))
+
+    def multiply(h):
+        own_half = dot_t(x_all[h * hr : (h + 1) * hr], e_all[h * hr : (h + 1) * hr])
+        for i in range(8):
+            sb[i, h].wait_recv()
+        lo = rows + h * hr
+        return own_half + dot_t(x_all[lo : lo + hr], e_all[lo : lo + hr])
 
     pass_on(0)
     for cp in ycs:
@@ -235,10 +239,9 @@
             )
     dms.append(remote(d_src, dm.at[1, var], dm_s.at[14], dm_r.at[14], sib))
 
+    cross[...] = multiply(0)
     pass_on(1)
-    for cp in sb.values():
-        cp.wait_recv()
-    cross[...] = dot_t(x_all[...], e_all[...])
+    cross[...] += multiply(1)
     for cp in dms:
         cp.wait_recv()
 
@@ -309,8 +312,11 @@
         for n in (5, 6, 3, 4):
             zx[i, n].wait_recv()
             acc = acc + zx_buf[i, n].astype(F32)
-        ysrc[i, 0] = acc[:8]
-        ysrc[i, 1] = acc[8:]
+        if dy == 0:
+            own_y[0] = acc[:8]
+            own_y[1] = acc[8:]
+        ysrc[i, 0] = acc[:8].astype(BF16)
+        ysrc[i, 1] = acc[8:].astype(BF16)
         for dc in (1, 0):
             if dy or dc:
                 m = YC.index((dy, dc))
@@ -331,13 +337,13 @@
 
     for cp in yx:
         cp.wait_recv()
-    same = ysrc[len(DY) - 1, c]
+    same = own_y[c]
     cross_half = jnp.zeros_like(same)
     for i, (dy, dc) in enumerate(YC):
         if dc:
-            cross_half = cross_half + yx_buf[i]
+            cross_half = cross_half + yx_buf[i].astype(F32)
         else:
-            same = same + yx_buf[i]
+            same = same + yx_buf[i].astype(F32)
     o_ref[:, pl.ds(mine, half)] = same * scale
     o_ref[:, pl.ds(other, half)] = cross_half * scale
 
@@ -357,11 +363,11 @@
     scratch = [
         vm((rows, depth), BF16), vm((depth, k), BF16), vm((width, rows), F32), vm((2, 1, rows), jnp.int32),
         vm((2 * rows, half), BF16), vm((3 * width + 4 * COHORTS, rows), BF16), vm((3 * width + 4 * COHORTS, k), BF16),
-        vm((rows, k), BF16), vm((2 * blk, k), F32), vm((7, 2, blk // 2, k), BF16), vm((2 * rows, k), BF16),
+        vm((2, rows // 2, k), BF16), vm((2, rows // 2, k), F32), vm((7, 2, blk // 2, k), BF16), vm((2 * rows, k), BF16),
         vm((8, COHORTS, 128), F32), vm((7, COHORTS, 128), F32), vm((COHORTS, 128), F32), vm((7, COHORTS, 128), F32),
         vm((COHORTS, 128), F32), vm((7, COHORTS, 128), F32),
         vm((COHORTS, 128), F32), vm((2, 8, COHORTS, 128), F32), vm((k, half), F32), vm((k, half), BF16),
-        vm((4, 7, k // 32, half), BF16), vm((4, 2, k // 32, half), BF16), vm((4, 2, out_rows, half), F32), vm((7, out_rows, half), F32),
+        vm((4, 7, k // 32, half), BF16), vm((4, 2, k // 32, half), BF16), vm((2, out_rows, half), F32), vm((4, 2, out_rows, half), BF16), vm((7, out_rows, half), BF16),
         vm((8, 128), F32), vm((7, 8, 128), F32), vm((8, 128), F32), vm((7, 8, 128), F32),
         sem((5,)), sem((4,)), sem((7,)), sem((7,)), sem((7,)), sem((7,)), sem((7,)), sem((7,)),
         sem((15,)), sem((15,)), sem((7, 2)), sem((7, 2)), sem((7, 2)), sem((7, 2)), sem((8, 2)), sem((8, 2)),

time: 55.4 us -> 54.7 us (0.987)
  Pallas kernels: 53.8 us -> 53.1 us
    pallas_call x1, Pallas kernels: 53.8 us -> 53.1 us  [shards(): pl.pallas_call(functools.partial(kernel, float(total)), out_shape=jax.Sha...]
where the time goes in v4:
time: 54.7 us; the launch traced here: 54.5 us
  Pallas kernels  53.1 us (97%)
  local copies, waits for them, and re-layouts  1.4 us (3%)
    pallas_call x1, Pallas kernels, shards(): pl.pallas_call(functools.partial(kernel, float(total)), out_shape=jax.Sha...  53.1 us
    unnamed x1, local copies, waits for them, and re-layouts  1.4 us

profile of v4, /device:TPU:1, one launch (start us, length us, event | category | flops | bytes accessed | tf_op | source)
XLA Modules:
  0.0 54.5 jit_solution(3579197800557731831)
XLA Ops:
  0.0 53.1 %shard_map.55 = f32[8,1280]{1,0:T(8,128)} custom-call(bf16[512,1792]{1,0:T(8,128)(2,1)} %d_hbm.1, bf16[1792,512]{1,0:T(8,128)(2,1)} %w_hbm.1, f32[64,512]{1,0:T(8,128)} %bitcast.2, s32[1,512]{1,0:T(1,128)} %bitcast.3, bf16[512,1280]{1,0:T(8,128)(2,1)} %e_hbm.1), custom_call_target="tpu_custom_call" | custom-call | tf_op jit(solution)/shard_map/pallas_call | solution.py:376
  53.1 1.4 %copy.7 = f32[8,1280]{1,0:T(8,128)} copy(f32[8,1280]{1,0:T(8,128)} %shard_map.55) | data formatting | bytes 81920

commit v5 on v4

--- a/solution.py
+++ b/solution.py
@@ -196,7 +196,6 @@
             x_all.at[pl.ds(row, hb)], x_all.at[pl.ds(pl.multiple_of(rows + row, hb), hb)], sb_s.at[i, h], sb_r.at[i, h], sib
         )
 
-    spread_part(0)
     for cp in zs:
         cp.wait_recv()
     t2 = t
@@ -206,6 +205,7 @@
     ycs = [
         remote(t2_src, yc_buf.at[i], yc_s.at[i], yc_r.at[i], (samp_of(0, *q), var)) for i, q in enumerate(YC)
     ]
+    spread_part(0)
     spread_part(1)
 
     def pass_on(h):
@@ -269,14 +269,24 @@
         )
 
     zx = {}
-    for i, dy in enumerate(DY):
+
+    def far_blocks(i):
+        dy = DY[i]
         turn = 1 if i % 2 == 0 else -1
         zx[i, 0] = hop(i, 0, 2 * turn, cb.at[chunk_rows(z + 4, dy)])
         zx[i, 1] = hop(i, 1, 1, cb.at[chunk_rows(z + 3, dy)])
         zx[i, 2] = hop(i, 2, -1, cb.at[chunk_rows(z + NZ - 3, dy)])
-    for i, dy in enumerate(DY):
+
+    def near_blocks(i):
+        dy = DY[i]
         zx[i, 5] = hop(i, 5, 1, cb.at[chunk_rows(z + 1, dy)])
         zx[i, 6] = hop(i, 6, -1, cb.at[chunk_rows(z + NZ - 1, dy)])
+
+    for i in range(3):
+        far_blocks(i)
+    for i in range(3):
+        near_blocks(i)
+    far_blocks(3)
 
     xo = x_all[pl.ds(0, rows)]
     xf = xo.astype(F32)
@@ -297,6 +307,7 @@
                 part = part + zx_buf[i, 0].astype(F32)
             zx_src[i, a] = part.astype(BF16)
             zx[i, 3 + a] = hop(i, 3 + a, 2 * way, zx_src.at[i, a])
+    near_blocks(3)
     for cp in qy:
         cp.wait_recv()
     q2 = q_src[...]

time: 54.7 us -> 54.2 us (level)
  no operation moved by 1% of the time
where the time goes in v5:
time: 54.2 us; the launch traced here: 54 us
  Pallas kernels  52.6 us (97%)
  local copies, waits for them, and re-layouts  1.4 us (3%)
    pallas_call x1, Pallas kernels, shards(): pl.pallas_call(functools.partial(kernel, float(total)), out_shape=jax.Sha...  52.6 us
    unnamed x1, local copies, waits for them, and re-layouts  1.4 us

profile of v5, /device:TPU:1, one launch (start us, length us, event | category | flops | bytes accessed | tf_op | source)
XLA Modules:
  0.0 54.0 jit_solution(18252957927258029490)
XLA Ops:
  0.0 52.6 %shard_map.55 = f32[8,1280]{1,0:T(8,128)} custom-call(bf16[512,1792]{1,0:T(8,128)(2,1)} %d_hbm.1, bf16[1792,512]{1,0:T(8,128)(2,1)} %w_hbm.1, f32[64,512]{1,0:T(8,128)} %bitcast.2, s32[1,512]{1,0:T(1,128)} %bitcast.3, bf16[512,1280]{1,0:T(8,128)(2,1)} %e_hbm.1), custom_call_target="tpu_custom_call" | custom-call | tf_op jit(solution)/shard_map/pallas_call | solution.py:387
  52.6 1.4 %copy.7 = f32[8,1280]{1,0:T(8,128)} copy(f32[8,1280]{1,0:T(8,128)} %shard_map.55) | data formatting | bytes 81920
